TPU v7x, 256 devices: a whole 4x4x8 slice. The times are simulated.
256 devices in a mesh: cplx: 4 (over y_hi, core), row: 64 (over z, x, y_lo).
Axes of the slice: x: 4, y: 4 (y_hi: 2, y_lo: 2; y = y_hi * 2 + y_lo), z: 8, core: 2. Of those that a mesh axis runs over, the one named last changes fastest.
Arguments:
- pair_state: bfloat16 [2048, 512, 128], P(('cplx', 'row')), parts along dimension 0, may hold values from -60 to 60
- cotangent: bfloat16 [2048, 512, 128], P(('cplx', 'row')), parts along dimension 0, may hold values from -6 to 6
- token_mask: int32 [2048], P('cplx'), parts along dimension 0, may hold values 0 or 1
- input_gain: float32 [128], replicated, may hold values from 0.25 to 1.75
- input_bias: float32 [128], replicated, may hold values from -3 to 3
- input_weight: bfloat16 [128, 640], replicated, may hold values from -0.5 to 0.5
- output_gain: float32 [128], replicated, may hold values from 0.25 to 1.75
- output_bias: float32 [128], replicated, may hold values from -3 to 3
- output_weight: bfloat16 [128, 128], replicated, may hold values from -0.5 to 0.5
Outputs:
- pair_gradient: bfloat16 [2048, 512, 128], P(('cplx', 'row')), parts along dimension 0
- input_gradient: float32 [512, 640], P(('cplx', 'row')), parts along dimension 0
- output_gradient: float32 [512, 128], P(('cplx', 'row')), parts along dimension 0
There are 4 independent parts, one for each index of `cplx`. A program takes and returns all parts, laid end to end along the dimension named above; an argument that names none is the same for every part. Nothing has to cross between parts.
Inputs may be any that keep to these rules, and one draw needn't show every extreme that they name: `token_mask`: 1 marks a token of the complex, 0 a padding slot.
All inputs are finite; a program needn't handle non-finite values.
Results may differ from a plain program's by a relative error of at most 0.0076.
Values may be sent and summed in bfloat16 or wider, within the bound.
No kernel may reach another device: no remote copies, remote signals or barrier semaphores. Data moves between devices by JAX's collectives and lax.ppermute only.
A program may use at most 64 MiB of HBM per device.

v0:
```python
import jax
import jax.numpy as jnp
from jax import lax
from jax.sharding import PartitionSpec as P

epsilon = 1e-05


def norm_parts(values, norm_axis):
    average = jnp.mean(values, axis=norm_axis, keepdims=True)
    centered = values - average
    variance = jnp.mean(centered * centered, axis=norm_axis, keepdims=True)
    inverse = lax.rsqrt(variance + epsilon)
    return (centered * inverse, inverse)


def norm_backward(upstream, scaled, inverse, norm_axis):
    first_mean = jnp.mean(upstream, axis=norm_axis, keepdims=True)
    second = jnp.mean(upstream * scaled, axis=norm_axis, keepdims=True)
    return inverse * (upstream - first_mean - scaled * second)


def to_pieces(values, slab_count):
    return values.reshape(
        slab_count, values.shape[0] // slab_count, values.shape[1], values.shape[2]
    )


def from_pieces(values):
    return values.reshape(values.shape[0] * values.shape[1], values.shape[2], values.shape[3])


def triangle(left_slab, right_slab):
    result = jnp.einsum(
        "xcik,xcjk->xcij", left_slab, right_slab, preferred_element_type=jnp.float32
    )
    return result.astype(jnp.bfloat16)


def factor_gradients(grad_slab, left_slab, right_slab):
    left_part = jnp.einsum(
        "xcij,xcjk->xcik", grad_slab, right_slab, preferred_element_type=jnp.float32
    )
    right_part = jnp.einsum(
        "xcij,xcik->xcjk", grad_slab, left_slab, preferred_element_type=jnp.float32
    )
    return (left_part.astype(jnp.bfloat16), right_part.astype(jnp.bfloat16))


def project(normed, weight_block):
    return jnp.einsum("rnd,de->ern", normed, weight_block, preferred_element_type=jnp.float32)


def on_device(
    pair_state,
    cotangent,
    token_mask,
    input_gain,
    input_bias,
    input_weight,
    output_gain,
    output_bias,
    output_weight,
):
    row_count = pair_state.shape[0]
    tokens = pair_state.shape[1]
    channels = pair_state.shape[2]
    slab_count = lax.axis_size("row")
    token_float = token_mask.astype(jnp.float32)
    row_start = lax.axis_index("row") * row_count
    row_float = lax.dynamic_slice_in_dim(token_float, row_start, row_count)
    pair_mask = (row_float[:, None] * token_float[None, :])[None]
    scaled_in, inverse_in = norm_parts(pair_state.astype(jnp.float32), 2)
    normed = (scaled_in * input_gain + input_bias).astype(jnp.bfloat16)
    left_proj = project(normed, input_weight[:, 0 : 2 * channels])
    right_proj = project(normed, input_weight[:, 2 * channels : 4 * channels])
    out_gate = jax.nn.sigmoid(project(normed, input_weight[:, 4 * channels :]))
    left_lin = left_proj[:channels]
    left_gate = jax.nn.sigmoid(left_proj[channels:])
    right_lin = right_proj[:channels]
    right_gate = jax.nn.sigmoid(right_proj[channels:])
    left_rows = to_pieces((pair_mask * left_gate * left_lin).astype(jnp.bfloat16), slab_count)
    right_rows = to_pieces((pair_mask * right_gate * right_lin).astype(jnp.bfloat16), slab_count)
    left_slab, right_slab = (
        lax.all_to_all(left_rows, "row", split_axis=0, concat_axis=2, tiled=True),
        lax.all_to_all(right_rows, "row", split_axis=0, concat_axis=2, tiled=True),
    )
    product_slab = triangle(left_slab, right_slab)
    product_pieces = lax.all_to_all(product_slab, "row", split_axis=2, concat_axis=0, tiled=True)
    product_rows = from_pieces(product_pieces).astype(jnp.float32)
    scaled_out, inverse_out = norm_parts(product_rows, 0)
    normed_out = (scaled_out * output_gain[:, None, None] + output_bias[:, None, None]).astype(
        jnp.bfloat16
    )
    projected = jnp.einsum(
        "crn,cd->drn", normed_out, output_weight, preferred_element_type=jnp.float32
    )
    upstream = jnp.transpose(cotangent, (2, 0, 1)).astype(jnp.float32)
    mixed_grad = (upstream * out_gate).astype(jnp.bfloat16)
    gate_grad = upstream * projected * out_gate * (1.0 - out_gate)
    out_norm_grad = jnp.einsum(
        "drn,cd->crn", mixed_grad, output_weight, preferred_element_type=jnp.float32
    )
    product_grad = norm_backward(
        out_norm_grad * output_gain[:, None, None], scaled_out, inverse_out, 0
    ).astype(jnp.bfloat16)
    grad_rows = to_pieces(product_grad, slab_count)
    grad_slab = lax.all_to_all(grad_rows, "row", split_axis=0, concat_axis=2, tiled=True)
    left_part, right_part = factor_gradients(grad_slab, left_slab, right_slab)
    left_pieces, right_pieces = (
        lax.all_to_all(left_part, "row", split_axis=2, concat_axis=0, tiled=True),
        lax.all_to_all(right_part, "row", split_axis=2, concat_axis=0, tiled=True),
    )
    left_back = from_pieces(left_pieces).astype(jnp.float32) * pair_mask
    right_back = from_pieces(right_pieces).astype(jnp.float32) * pair_mask
    proj_grad = jnp.concatenate(
        [
            (left_back * left_gate).astype(jnp.bfloat16),
            (left_back * left_lin * left_gate * (1.0 - left_gate)).astype(jnp.bfloat16),
            (right_back * right_gate).astype(jnp.bfloat16),
            (right_back * right_lin * right_gate * (1.0 - right_gate)).astype(jnp.bfloat16),
            gate_grad.astype(jnp.bfloat16),
        ],
        axis=0,
    )
    normed_grad = jnp.einsum(
        "ern,de->rnd", proj_grad, input_weight, preferred_element_type=jnp.float32
    )
    pair_gradient = norm_backward(normed_grad * input_gain, scaled_in, inverse_in, 2).astype(
        jnp.bfloat16
    )
    input_term = (
        jnp.einsum("rnd,ern->de", normed, proj_grad, preferred_element_type=jnp.float32) / tokens
    )
    output_term = (
        jnp.einsum("crn,drn->cd", normed_out, mixed_grad, preferred_element_type=jnp.float32)
        / tokens
    )
    input_gradient, output_gradient = (
        lax.psum_scatter(input_term, "row", scatter_dimension=0, tiled=True),
        lax.psum_scatter(output_term, "row", scatter_dimension=0, tiled=True),
    )
    return (pair_gradient, input_gradient, output_gradient)


def solution(mesh):
    return jax.shard_map(
        on_device,
        mesh=mesh,
        in_specs=(
            P(("cplx", "row"), None, None),
            P(("cplx", "row"), None, None),
            P("cplx"),
            P(),
            P(),
            P(),
            P(),
            P(),
            P(),
        ),
        out_specs=(
            P(("cplx", "row"), None, None),
            P(("cplx", "row"), None),
            P(("cplx", "row"), None),
        ),
        check_vma=False,
    )
```

profile of v0, /device:TPU:16, one launch (start us, length us, event | category | flops | bytes accessed | tf_op | source)
XLA Modules:
  0.0 879.4 jit_solution(5712075969375751696)
XLA Ops:
  9.3 2.7 convolution_bitcast_fusion
  12.1 2.8 convolution_bitcast_fusion.1
  15.0 4.7 multiply_convert_fusion.5
  21.0 3.4 copy.32
  24.4 12.9 %all-to-all-start = ((bf16[64,2,8,512]{3,1,2,0:T(2,128)(2,1)}), bf16[64,2,8,512]{3,1,2,0:T(2,128)(2,1)}, u32[]{:S(2)}, u32[]{:S(2)}) async-start(bf16[64,2,8,512]{3,1,2,0:T(2,128)(2,1)} %copy.32), calls=%async_computation | async-start | bytes 2097152 | tf_op jit(solution)/shard_map/all_to_all | solution.py:85
  38.9 27.1 %all-to-all-done = bf16[64,2,8,512]{3,1,2,0:T(2,128)(2,1)} async-done(((bf16[64,2,8,512]{3,1,2,0:T(2,128)(2,1)}), bf16[64,2,8,512]{3,1,2,0:T(2,128)(2,1)}, u32[]{:S(2)}, u32[]{:S(2)}) %all-to-all-start) | async-done | bytes 1048608 | tf_op jit(solution)/shard_map/all_to_all | solution.py:85
  66.0 34.1 %all_to_all.72 = bf16[64,2,8,512]{3,1,2,0:T(2,128)(2,1)S(1)} all-to-all(bf16[64,2,8,512]{3,1,2,0:T(2,128)(2,1)S(1)} %copy.36), channel_id=1, replica_groups=mesh['cplx'=4,'row'=64] {'row'}, dimensions={0} | all-to-all | bytes 2097152 | tf_op jit(solution)/shard_map/all_to_all | solution.py:86
  105.2 5.8 all-to-all-start.2
  112.3 2.3 add_divide_fusion
  114.6 24.3 %all-to-all-done.2 = bf16[1,2,512,512]{3,1,0,2:T(2,128)(2,1)S(1)} async-done(((bf16[1,2,512,512]{3,1,0,2:T(2,128)(2,1)}), bf16[1,2,512,512]{3,1,0,2:T(2,128)(2,1)S(1)}, u32[]{:S(2)}, u32[]{:S(2)}) %all-to-all-start.2) | async-done | bytes 1048608 | tf_op jit(solution)/shard_map/all_to_all | solution.py:89
  141.8 2.7 reshape.136
  144.6 2.6 multiply_reduce_fusion
  147.2 2.7 bitcast_reduce_fusion
  153.8 2.4 copy.43
  156.2 33.4 %all_to_all.73 = bf16[64,2,8,512]{3,1,2,0:T(2,128)(2,1)S(1)} all-to-all(bf16[64,2,8,512]{3,1,2,0:T(2,128)(2,1)S(1)} %copy.43), channel_id=1, replica_groups=mesh['cplx'=4,'row'=64] {'row'}, dimensions={0} | all-to-all | bytes 2097152 | tf_op jit(solution)/shard_map/all_to_all | solution.py:108
  194.6 6.2 all-to-all-start.5
  200.9 2.3 fusion.28
  205.2 23.1 %all-to-all-done.5 = bf16[1,2,512,512]{3,1,0,2:T(2,128)(2,1)} async-done(((bf16[1,2,512,512]{3,1,0,2:T(2,128)(2,1)}), bf16[1,2,512,512]{3,1,0,2:T(2,128)(2,1)}, u32[]{:S(2)}, u32[]{:S(2)}) %all-to-all-start.5) | async-done | bytes 1048608 | tf_op jit(solution)/shard_map/all_to_all | solution.py:112
  228.3 6.0 all-to-all-start.4
  235.7 3.1 fusion.31
  238.8 3.3 copy_bitcast_fusion
  242.1 3.7 reshape.138
  245.8 16.2 %all-to-all-done.4 = bf16[1,2,512,512]{3,1,0,2:T(2,128)(2,1)} async-done(((bf16[1,2,512,512]{3,1,0,2:T(2,128)(2,1)}), bf16[1,2,512,512]{3,1,0,2:T(2,128)(2,1)}, u32[]{:S(2)}, u32[]{:S(2)}) %all-to-all-start.4) | async-done | bytes 1048608 | tf_op jit(solution)/shard_map/all_to_all | solution.py:111
  262.0 3.3 copy_bitcast_fusion.1
  265.3 3.6 reshape.137
  269.0 3.0 fusion.32
  272.4 2.6 fusion.33
  279.3 2.3 copy-done.7
  281.6 2.5 fusion.30
  284.1 3.5 multiply_reduce_fusion.1
  289.2 2.3 copy.51
  291.5 578.5 %all-reduce.5.cloned.1.call-done = (f32[128,640]{1,0:T(8,128)}, f32[128,128]{1,0:T(8,128)}) async-done(((f32[128,640]{1,0:T(8,128)}, f32[128,128]{1,0:T(8,128)}), (f32[128,640]{1,0:T(8,128)}, f32[128,128]{1,0:T(8,128)})) %all-reduce.5.cloned.1.call-update) | async-done | bytes 393232
  (70 shorter events, 34.7 us)
Async XLA Ops:
  7.2 140.0 %copy-start = (bf16[128,128]{1,0:T(8,128)(2,1)S(1)}, bf16[128,128]{1,0:T(8,128)(2,1)}, u32[]{:S(2)}) copy-start(bf16[128,128]{1,0:T(8,128)(2,1)} %param.17) | copy-start | bytes 98308
  7.2 2.1 copy-start.12
  7.2 2.1 copy-start.14
  7.2 2.1 copy-start.11
  12.1 2.8 copy-start.15
  24.4 41.6 %all-to-all-start = ((bf16[64,2,8,512]{3,1,2,0:T(2,128)(2,1)}), bf16[64,2,8,512]{3,1,2,0:T(2,128)(2,1)}, u32[]{:S(2)}, u32[]{:S(2)}) async-start(bf16[64,2,8,512]{3,1,2,0:T(2,128)(2,1)} %copy.32), calls=%async_computation | async-start | bytes 2097152 | tf_op jit(solution)/shard_map/all_to_all | solution.py:85
  100.1 1.0 copy-start.9
  103.1 7.9 copy-start.8
  105.2 33.7 %all-to-all-start.2 = ((bf16[1,2,512,512]{3,1,0,2:T(2,128)(2,1)}), bf16[1,2,512,512]{3,1,0,2:T(2,128)(2,1)S(1)}, u32[]{:S(2)}, u32[]{:S(2)}) async-start(bf16[1,2,512,512]{3,1,0,2:T(2,128)(2,1)} %copy.38), calls=%async_computation.2 | async-start | bytes 2097152 | tf_op jit(solution)/shard_map/all_to_all | solution.py:89
  138.9 2.1 copy-start.5
  141.8 5.4 copy-start.13
  189.6 1.0 copy-start.10
  194.6 33.7 %all-to-all-start.5 = ((bf16[1,2,512,512]{3,1,0,2:T(2,128)(2,1)}), bf16[1,2,512,512]{3,1,0,2:T(2,128)(2,1)}, u32[]{:S(2)}, u32[]{:S(2)}) async-start(bf16[1,2,512,512]{3,1,0,2:T(2,128)(2,1)} %copy.48), calls=%async_computation.5 | async-start | bytes 2097152 | tf_op jit(solution)/shard_map/all_to_all | solution.py:112
  203.1 31.3 %copy-start.17 = (u32[256]{0:T(256)S(1)}, u32[256]{0:T(256)}, u32[]{:S(2)}) copy-start(u32[256]{0:T(256)} %constant.37) | copy-start | bytes 3076
  203.1 32.5 %copy-start.16 = (f32[128]{0:T(128)S(1)}, f32[128]{0:T(128)}, u32[]{:S(2)}) copy-start(f32[128]{0:T(128)} %param.16) | copy-start | bytes 1540
  228.3 33.7 %all-to-all-start.4 = ((bf16[1,2,512,512]{3,1,0,2:T(2,128)(2,1)}), bf16[1,2,512,512]{3,1,0,2:T(2,128)(2,1)}, u32[]{:S(2)}, u32[]{:S(2)}) async-start(bf16[1,2,512,512]{3,1,0,2:T(2,128)(2,1)} %copy.45), calls=%async_computation.4 | async-start | bytes 2097152 | tf_op jit(solution)/shard_map/all_to_all | solution.py:111
  234.4 635.6 %all-reduce.5.cloned.1.call-start = ((), (), s32[]{:S(2)}) async-start(), calls=%async_computation.6 | async-start | bytes 786432
  269.0 3.4 copy-start.2
  272.4 2.8 copy-start.1
  272.4 3.5 copy-start.3
  276.6 1.6 copy-start.4
  276.6 1.8 copy-start.6
  279.3 2.3 copy-start.7
Sparse Core Ops, SparseCore 0:
  287.8 582.1 all-reduce.4
where the time goes:
time: 880 us; the launch traced here: 879 us
  waiting for transfers between devices  669 us (76%)
  blocking collectives  67.5 us (8%)
  local copies, waits for them, and re-layouts  41.9 us (5%)
  starting transfers between devices  31.1 us (4%)
  other arithmetic  27.9 us (3%)
  matrix products  26.7 us (3%)
  between operations  15.1 us (2%)
    unnamed x2, waiting for transfers between devices  578 us
    all_to_all x1, blocking collectives, on_device(): lax.all_to_all(right_rows, 'row', split_axis=0, concat_axis=2, tiled=True)  34.1 us
    all_to_all x1, blocking collectives, on_device(): lax.all_to_all(grad_rows, 'row', split_axis=0, concat_axis=2, tiled=True)  33.4 us
    all_to_all x1, waiting for transfers between devices, on_device(): lax.all_to_all(left_rows, 'row', split_axis=0, concat_axis=2, tiled=True)  27.1 us
    all_to_all x1, waiting for transfers between devices, on_device(): lax.all_to_all(product_slab, 'row', split_axis=2, concat_axis=0, tiled=True)  24.3 us
    all_to_all x1, waiting for transfers between devices, on_device(): lax.all_to_all(right_part, 'row', split_axis=2, concat_axis=0, tiled=True)  23.1 us
  transfers between devices with their start and end apart: 5, of which 5 were waited for; matrix products, arithmetic and copies ran while one was open for 3% of the time, Pallas kernels for 0%

commit v1 on v0

--- a/solution.py
+++ b/solution.py
@@ -82,7 +82,12 @@
     left_rows = to_pieces((pair_mask * left_gate * left_lin).astype(jnp.bfloat16), slab_count)
     right_rows = to_pieces((pair_mask * right_gate * right_lin).astype(jnp.bfloat16), slab_count)
     left_slab, right_slab = (
-        lax.all_to_all(left_rows, "row", split_axis=0, concat_axis=2, tiled=True),
+        jnp.concatenate(
+            lax.all_to_all(
+                jnp.stack(jnp.split(left_rows, lax.axis_size("row"), axis=0)), "row", 0, 0
+            ),
+            axis=2,
+        ),
         lax.all_to_all(right_rows, "row", split_axis=0, concat_axis=2, tiled=True),
     )
     product_slab = triangle(left_slab, right_slab)

time: 880 us -> 922 us (1.048)
  local copies, waits for them, and re-layouts: 41.9 us -> 72.7 us
    unnamed x42 -> x101, local copies, waits for them, and re-layouts: 14.9 us -> 49.6 us
    all_to_all x1, waiting for transfers between devices: 23.1 us -> 8.82 us  [on_device(): lax.all_to_all(right_part, 'row', split_axis=2, concat_axis=0, tiled=True)]
where the time goes in v1:
time: 922 us; the launch traced here: 913 us
  waiting for transfers between devices  662 us (72%)
  local copies, waits for them, and re-layouts  72.7 us (8%)
  blocking collectives  67.5 us (7%)
  other arithmetic  34.7 us (4%)
  starting transfers between devices  31 us (3%)
  matrix products  29.1 us (3%)
  between operations  15.4 us (2%)
    unnamed x2, waiting for transfers between devices  578 us
    unnamed x101, local copies, waits for them, and re-layouts  49.6 us
    all_to_all x1, blocking collectives, on_device(): lax.all_to_all(right_rows, 'row', split_axis=0, concat_axis=2, tiled=True)  34.1 us
    all_to_all x1, blocking collectives, on_device(): lax.all_to_all(grad_rows, 'row', split_axis=0, concat_axis=2, tiled=True)  33.4 us
    all_to_all x1, waiting for transfers between devices, on_device(): lax.all_to_all(jnp.stack(jnp.split(left_rows, lax.axis_size('row'), axis=...  27.1 us
    all_to_all x1, waiting for transfers between devices, on_device(): lax.all_to_all(product_slab, 'row', split_axis=2, concat_axis=0, tiled=True)  24.5 us
    all_to_all x1, waiting for transfers between devices, on_device(): lax.all_to_all(left_part, 'row', split_axis=2, concat_axis=0, tiled=True)  23.3 us
  transfers between devices with their start and end apart: 5, of which 5 were waited for; matrix products, arithmetic and copies ran while one was open for 3% of the time, Pallas kernels for 0%

profile of v1, /device:TPU:16, one launch (start us, length us, event | category | flops | bytes accessed | tf_op | source)
XLA Modules:
  0.0 912.6 jit_solution(17831221057615042887)
XLA Ops:
  9.3 2.8 convolution_bitcast_fusion
  12.1 2.9 convolution_bitcast_fusion.1
  15.1 4.7 multiply_convert_fusion.4
  59.8 12.9 %all-to-all-start = ((bf16[64,1,2,8,512]{4,2,3,1,0:T(2,128)(2,1)}), bf16[64,1,2,8,512]{4,2,3,1,0:T(2,128)(2,1)}, u32[]{:S(2)}, u32[]{:S(2)}) async-start(bf16[64,1,2,8,512]{4,2,3,1,0:T(2,128)(2,1)} %constant_dynamic-update-slice_fusion), calls=%async_computation | async-start | bytes 2097152 | tf_op jit(solution)/shard_map/all_to_all | solution.py:86
  74.3 27.1 %all-to-all-done = bf16[64,1,2,8,512]{4,2,3,1,0:T(2,128)(2,1)} async-done(((bf16[64,1,2,8,512]{4,2,3,1,0:T(2,128)(2,1)}), bf16[64,1,2,8,512]{4,2,3,1,0:T(2,128)(2,1)}, u32[]{:S(2)}, u32[]{:S(2)}) %all-to-all-start) | async-done | bytes 1048608 | tf_op jit(solution)/shard_map/all_to_all | solution.py:86
  101.4 34.1 %all_to_all.62 = bf16[64,2,8,512]{3,1,2,0:T(2,128)(2,1)S(1)} all-to-all(bf16[64,2,8,512]{3,1,2,0:T(2,128)(2,1)S(1)} %copy.35), channel_id=1, replica_groups=mesh['cplx'=4,'row'=64] {'row'}, dimensions={0} | all-to-all | bytes 2097152 | tf_op jit(solution)/shard_map/all_to_all | solution.py:91
  140.5 5.8 all-to-all-start.2
  147.7 2.2 add_divide_fusion
  149.9 24.5 %all-to-all-done.2 = bf16[1,2,512,512]{3,1,0,2:T(2,128)(2,1)S(1)} async-done(((bf16[1,2,512,512]{3,1,0,2:T(2,128)(2,1)}), bf16[1,2,512,512]{3,1,0,2:T(2,128)(2,1)S(1)}, u32[]{:S(2)}, u32[]{:S(2)}) %all-to-all-start.2) | async-done | bytes 1048608 | tf_op jit(solution)/shard_map/all_to_all | solution.py:94
  178.8 2.7 reshape.266
  181.5 2.7 bitcast_reduce_fusion
  185.8 2.2 reshape.264
  188.1 2.5 copy.43
  190.5 33.4 %all_to_all.63 = bf16[64,2,8,512]{3,1,2,0:T(2,128)(2,1)S(1)} all-to-all(bf16[64,2,8,512]{3,1,2,0:T(2,128)(2,1)S(1)} %copy.43), channel_id=1, replica_groups=mesh['cplx'=4,'row'=64] {'row'}, dimensions={0} | all-to-all | bytes 2097152 | tf_op jit(solution)/shard_map/all_to_all | solution.py:113
  227.7 6.2 all-to-all-start.4
  234.0 2.3 fusion.29
  238.4 23.3 %all-to-all-done.4 = bf16[1,2,512,512]{3,1,0,2:T(2,128)(2,1)} async-done(((bf16[1,2,512,512]{3,1,0,2:T(2,128)(2,1)}), bf16[1,2,512,512]{3,1,0,2:T(2,128)(2,1)}, u32[]{:S(2)}, u32[]{:S(2)}) %all-to-all-start.4) | async-done | bytes 1048608 | tf_op jit(solution)/shard_map/all_to_all | solution.py:116
  261.7 6.0 all-to-all-start.5
  269.0 3.1 fusion.31
  272.1 3.3 copy_bitcast_fusion.1
  275.5 3.7 reshape.267
  279.1 4.0 fusion.32
  283.1 3.4 fusion.33
  286.5 8.8 all-to-all-done.5
  295.3 3.4 copy_bitcast_fusion
  298.8 3.6 reshape.268
  302.4 4.1 fusion.34
  306.5 3.6 fusion.35
  312.0 3.5 multiply_reduce_fusion.1
  315.5 5.0 fusion.30
  322.1 2.3 copy.52
  324.4 578.5 %all-reduce.5.cloned.1.call-done = (f32[128,640]{1,0:T(8,128)}, f32[128,128]{1,0:T(8,128)}) async-done(((f32[128,640]{1,0:T(8,128)}, f32[128,128]{1,0:T(8,128)}), (f32[128,640]{1,0:T(8,128)}, f32[128,128]{1,0:T(8,128)})) %all-reduce.5.cloned.1.call-update) | async-done | bytes 393232
  (128 shorter events, 68.6 us)
Async XLA Ops:
  7.2 174.3 %copy-start = (bf16[128,128]{1,0:T(8,128)(2,1)S(1)}, bf16[128,128]{1,0:T(8,128)(2,1)}, u32[]{:S(2)}) copy-start(bf16[128,128]{1,0:T(8,128)(2,1)} %param.17) | copy-start | bytes 98308
  7.2 2.1 copy-start.9
  7.2 2.1 copy-start.10
  7.2 2.1 copy-start.12
  12.1 2.9 copy-start.13
  59.8 41.6 %all-to-all-start = ((bf16[64,1,2,8,512]{4,2,3,1,0:T(2,128)(2,1)}), bf16[64,1,2,8,512]{4,2,3,1,0:T(2,128)(2,1)}, u32[]{:S(2)}, u32[]{:S(2)}) async-start(bf16[64,1,2,8,512]{4,2,3,1,0:T(2,128)(2,1)} %constant_dynamic-update-slice_fusion), calls=%async_computation | async-start | bytes 2097152 | tf_op jit(solution)/shard_map/all_to_all | solution.py:86
  135.5 1.0 copy-start.6
  138.4 7.9 copy-start.5
  140.5 33.9 %all-to-all-start.2 = ((bf16[1,2,512,512]{3,1,0,2:T(2,128)(2,1)}), bf16[1,2,512,512]{3,1,0,2:T(2,128)(2,1)S(1)}, u32[]{:S(2)}, u32[]{:S(2)}) async-start(bf16[1,2,512,512]{3,1,0,2:T(2,128)(2,1)} %copy.38), calls=%async_computation.2 | async-start | bytes 2097152 | tf_op jit(solution)/shard_map/all_to_all | solution.py:94
  178.7 2.7 copy-start.11
  188.1 36.9 %copy-start.7 = (bf16[64,2,8,512]{3,1,2,0:T(2,128)(2,1)S(1)}, bf16[64,2,8,512]{3,1,2,0:T(2,128)(2,1)}, u32[]{:S(2)}) copy-start(bf16[64,2,8,512]{3,1,2,0:T(2,128)(2,1)} %copy-done.6) | copy-start | bytes 3145732
  224.0 1.0 copy-start.8
  227.7 33.9 %all-to-all-start.4 = ((bf16[1,2,512,512]{3,1,0,2:T(2,128)(2,1)}), bf16[1,2,512,512]{3,1,0,2:T(2,128)(2,1)}, u32[]{:S(2)}, u32[]{:S(2)}) async-start(bf16[1,2,512,512]{3,1,0,2:T(2,128)(2,1)} %copy.45), calls=%async_computation.4 | async-start | bytes 2097152 | tf_op jit(solution)/shard_map/all_to_all | solution.py:116
  236.3 31.5 %copy-start.15 = (u32[256]{0:T(256)S(1)}, u32[256]{0:T(256)}, u32[]{:S(2)}) copy-start(u32[256]{0:T(256)} %constant.37) | copy-start | bytes 3076
  236.3 32.7 %copy-start.14 = (f32[128]{0:T(128)S(1)}, f32[128]{0:T(128)}, u32[]{:S(2)}) copy-start(f32[128]{0:T(128)} %param.16) | copy-start | bytes 1540
  261.7 33.7 %all-to-all-start.5 = ((bf16[1,2,512,512]{3,1,0,2:T(2,128)(2,1)}), bf16[1,2,512,512]{3,1,0,2:T(2,128)(2,1)}, u32[]{:S(2)}, u32[]{:S(2)}) async-start(bf16[1,2,512,512]{3,1,0,2:T(2,128)(2,1)} %copy.49), calls=%async_computation.5 | async-start | bytes 2097152 | tf_op jit(solution)/shard_map/all_to_all | solution.py:117
  267.7 635.1 %all-reduce.5.cloned.1.call-start = ((), (), s32[]{:S(2)}) async-start(), calls=%async_computation.6 | async-start | bytes 786432
  279.1 4.0 copy-start.2
  302.4 4.1 copy-start.1
  306.5 3.6 copy-start.3
  306.5 3.6 copy-start.4
Sparse Core Ops, SparseCore 0:
  320.6 582.1 all-reduce.4
